TPU v7x, 32 devices: a whole 2x2x4 slice. The times are simulated.
32 devices in a mesh: dp: 2 (over y), head: 16 (over z, x, core).
Axes of the slice: x: 2, y: 2, z: 4, core: 2. Of those that a mesh axis runs over, the one named last changes fastest.
Arguments:
- head_ids: int32 [2, 2048, 8], P('dp', 'head'), may hold values from 0 to 63, as said below
- query_slots: bfloat16 [2, 2048, 8, 128], P('dp', 'head'), may hold values from -300 to 300
- key_slots: bfloat16 [2, 2048, 8, 128], P('dp', 'head'), may hold values from -13 to 13
- value_slots: bfloat16 [2, 2048, 8, 128], P('dp', 'head'), may hold values from -5 to 5
- gate_logits: float32 [2, 2048, 8], P('dp', 'head'), may hold values from -8 to 310
- sink_logits: float32 [64], P('head'), may hold values from 1 to 6
- out_grad: bfloat16 [2, 2048, 8, 128], P('dp', 'head'), may hold values from -6 to 6
Outputs:
- mixed: bfloat16 [2, 2048, 8, 128], P('dp', 'head')
- query_grad: bfloat16 [2, 2048, 8, 128], P('dp', 'head')
- key_grad: bfloat16 [2, 2048, 8, 128], P('dp', 'head')
- value_grad: bfloat16 [2, 2048, 8, 128], P('dp', 'head')
- gate_grad: float32 [2, 2048, 8], P('dp', 'head')
- sink_grad: float32 [64], P('head')
Inputs may be any that keep to these rules, and one draw needn't show every extreme that they name: `head_ids`: each token names 8 different heads. Among the 128 tokens of one device no head is named more than 32 times, and in every group one head is named exactly 32 times by the tokens of every device of that group.
All inputs are finite; a program needn't handle non-finite values.
Results may differ from a plain program's by a relative error of at most 0.023.
Values may be sent and summed in bfloat16 or wider, within the bound.
No kernel may reach another device: no remote copies, remote signals or barrier semaphores. Data moves between devices by JAX's collectives and lax.ppermute only.
A program may use at most 64 MiB of HBM per device.

v0:
```python
import math
import jax
import jax.numpy as jnp
from jax import lax
from jax.sharding import PartitionSpec as P

HEADS = 64
BLOCK = 512
SLOT = 32
masked_value = -1e30


def block_scores(query_tile, key_tile, query_live, key_live, query_offset, key_offset, scale):
    scores = scale * jnp.einsum(
        "qd,kd->qk", query_tile, key_tile, preferred_element_type=jnp.float32
    )
    query_index = query_offset + lax.iota(jnp.int32, query_tile.shape[0])
    key_index = key_offset + lax.iota(jnp.int32, key_tile.shape[0])
    allowed = query_live[:, None] & key_live[None, :] & (key_index[None, :] <= query_index[:, None])
    return (scores, allowed)


def forward_head(query_rows, key_rows, value_rows, live_rows, sink_value, used_blocks, width):
    row_count, head_width = query_rows.shape
    scale = 1.0 / math.sqrt(head_width)

    def forward_query_block(qblock, carry):
        lse_all, out_all = carry
        offset = qblock * width
        query_tile = lax.dynamic_slice_in_dim(query_rows, offset, width, 0)
        query_live = lax.dynamic_slice_in_dim(live_rows, offset, width, 0)

        def tile_at(kblock):
            key_offset = kblock * width
            key_tile = lax.dynamic_slice_in_dim(key_rows, key_offset, width, 0)
            value_tile = lax.dynamic_slice_in_dim(value_rows, key_offset, width, 0)
            key_live = lax.dynamic_slice_in_dim(live_rows, key_offset, width, 0)
            scores, allowed = block_scores(
                query_tile, key_tile, query_live, key_live, offset, key_offset, scale
            )
            return (scores, allowed, value_tile)

        def stat_step(kblock, state):
            run_max, run_sum = state
            scores, allowed, value_tile = tile_at(kblock)
            masked = jnp.where(allowed, scores, masked_value)
            new_max = jnp.maximum(run_max, jnp.max(masked, axis=1))
            new_sum = run_sum * jnp.exp(run_max - new_max) + jnp.sum(
                jnp.where(allowed, jnp.exp(masked - new_max[:, None]), 0.0), axis=1
            )
            return (new_max, new_sum)

        start_state = (jnp.full((width,), sink_value, jnp.float32), jnp.ones((width,), jnp.float32))
        run_max, run_sum = lax.fori_loop(0, qblock + 1, stat_step, start_state)
        row_lse = run_max + jnp.log(run_sum)

        def value_step(kblock, total):
            scores, allowed, value_tile = tile_at(kblock)
            weights = jnp.where(allowed, jnp.exp(scores - row_lse[:, None]), 0.0).astype(
                jnp.bfloat16
            )
            return total + jnp.dot(weights, value_tile, preferred_element_type=jnp.float32)

        total = lax.fori_loop(
            0, qblock + 1, value_step, jnp.zeros((width, head_width), jnp.float32)
        )
        lse_all = lax.dynamic_update_slice_in_dim(lse_all, row_lse, offset, 0)
        out_all = lax.dynamic_update_slice_in_dim(out_all, total.astype(jnp.bfloat16), offset, 0)
        return (lse_all, out_all)

    start_all = (
        jnp.zeros((row_count,), jnp.float32),
        jnp.zeros((row_count, head_width), jnp.bfloat16),
    )
    return lax.fori_loop(0, used_blocks, forward_query_block, start_all)


def backward_head(
    query_rows,
    key_rows,
    value_rows,
    cot_rows,
    head_out,
    lse_all,
    live_rows,
    sink_value,
    used_blocks,
    width,
):
    row_count, head_width = query_rows.shape
    scale = 1.0 / math.sqrt(head_width)
    deltas = jnp.sum(cot_rows.astype(jnp.float32) * head_out.astype(jnp.float32), axis=1)
    sink_term = -jnp.sum(jnp.exp(sink_value - lse_all) * deltas)

    def backward_query_block(qblock, carry):
        qgrad_all, kgrad_acc, vgrad_acc = carry
        offset = qblock * width
        query_tile = lax.dynamic_slice_in_dim(query_rows, offset, width, 0)
        cot_tile = lax.dynamic_slice_in_dim(cot_rows, offset, width, 0)
        lse_tile = lax.dynamic_slice_in_dim(lse_all, offset, width, 0)
        delta_tile = lax.dynamic_slice_in_dim(deltas, offset, width, 0)
        query_live = lax.dynamic_slice_in_dim(live_rows, offset, width, 0)

        def key_step(kblock, inner):
            qgrad_run, kgrad_acc, vgrad_acc = inner
            key_offset = kblock * width
            key_tile = lax.dynamic_slice_in_dim(key_rows, key_offset, width, 0)
            value_tile = lax.dynamic_slice_in_dim(value_rows, key_offset, width, 0)
            key_live = lax.dynamic_slice_in_dim(live_rows, key_offset, width, 0)
            scores, allowed = block_scores(
                query_tile, key_tile, query_live, key_live, offset, key_offset, scale
            )
            probability = jnp.where(allowed, jnp.exp(scores - lse_tile[:, None]), 0.0)
            weights = probability.astype(jnp.bfloat16)
            dprob = jnp.einsum(
                "qd,kd->qk", cot_tile, value_tile, preferred_element_type=jnp.float32
            )
            dscore = (probability * (dprob - delta_tile[:, None])).astype(jnp.bfloat16)
            qgrad_run = qgrad_run + jnp.dot(dscore, key_tile, preferred_element_type=jnp.float32)
            kgrad_part = jnp.einsum(
                "qk,qd->kd", dscore, query_tile, preferred_element_type=jnp.float32
            )
            vgrad_part = jnp.einsum(
                "qk,qd->kd", weights, cot_tile, preferred_element_type=jnp.float32
            )
            kgrad_acc = lax.dynamic_update_slice_in_dim(
                kgrad_acc,
                lax.dynamic_slice_in_dim(kgrad_acc, key_offset, width, 0) + kgrad_part,
                key_offset,
                0,
            )
            vgrad_acc = lax.dynamic_update_slice_in_dim(
                vgrad_acc,
                lax.dynamic_slice_in_dim(vgrad_acc, key_offset, width, 0) + vgrad_part,
                key_offset,
                0,
            )
            return (qgrad_run, kgrad_acc, vgrad_acc)

        start_inner = (jnp.zeros((width, head_width), jnp.float32), kgrad_acc, vgrad_acc)
        qgrad_run, kgrad_acc, vgrad_acc = lax.fori_loop(0, qblock + 1, key_step, start_inner)
        qgrad_all = lax.dynamic_update_slice_in_dim(
            qgrad_all, (scale * qgrad_run).astype(jnp.bfloat16), offset, 0
        )
        return (qgrad_all, kgrad_acc, vgrad_acc)

    start_all = (
        jnp.zeros((row_count, head_width), jnp.bfloat16),
        jnp.zeros((row_count, head_width), jnp.float32),
        jnp.zeros((row_count, head_width), jnp.float32),
    )
    qgrad_all, kgrad_acc, vgrad_acc = lax.fori_loop(0, used_blocks, backward_query_block, start_all)
    return (
        qgrad_all,
        (scale * kgrad_acc).astype(jnp.bfloat16),
        vgrad_acc.astype(jnp.bfloat16),
        sink_term,
    )


def arrange(live_rows, width):
    row_count = live_rows.shape[0]
    return (None, None, row_count // width)


def pick_rows(buffer, head_slot):
    picked = buffer[:, head_slot].reshape(-1, buffer.shape[-1])
    return picked


def restore(row_block, devices):
    return row_block.reshape(devices, -1, row_block.shape[-1])


def per_device(head_ids, query_slots, key_slots, value_slots, gate_logits, sink_logits, out_grad):
    devices = lax.axis_size("head")
    local_heads = HEADS // devices
    selected = head_ids[0]
    token_count, slot_count = selected.shape
    head_width = query_slots.shape[-1]
    matches = (selected[:, :, None] == lax.iota(jnp.int32, HEADS)[None, None, :]).astype(jnp.int32)
    per_token = jnp.sum(matches, axis=1)
    earlier = jnp.cumsum(per_token, axis=0) - per_token
    placing = jnp.sum(matches * earlier[:, None, :], axis=2)
    target = (selected * SLOT + placing).reshape(-1)
    buffer_rows = HEADS * SLOT

    def spread_out(flat_rows):
        filled_rows = (
            jnp.zeros((buffer_rows, flat_rows.shape[-1]), flat_rows.dtype).at[target].set(flat_rows)
        )
        return filled_rows.reshape(devices, local_heads, SLOT, flat_rows.shape[-1])

    def collect(buffer):
        return buffer.reshape(buffer_rows, buffer.shape[-1])[target].reshape(
            token_count, slot_count, buffer.shape[-1]
        )

    gate_probs = jax.nn.softmax(gate_logits[0], axis=-1)
    cotangent = (gate_probs[:, :, None] * out_grad[0].astype(jnp.float32)).astype(jnp.bfloat16)
    send_query = spread_out(query_slots[0].reshape(-1, head_width))
    send_key = spread_out(key_slots[0].reshape(-1, head_width))
    send_value = spread_out(value_slots[0].reshape(-1, head_width))
    send_cot = spread_out(cotangent.reshape(-1, head_width))
    filled = (
        jnp.zeros((buffer_rows,), jnp.bfloat16)
        .at[target]
        .set(jnp.ones((), jnp.bfloat16))
        .reshape(devices, local_heads, SLOT)
    )
    out_list, qgrad_list, kgrad_list, vgrad_list, sink_list = ([], [], [], [], [])
    recv_query, recv_key, recv_value, recv_fill = (
        lax.all_to_all(send_query, "head", split_axis=0, concat_axis=0, tiled=True),
        lax.all_to_all(send_key, "head", split_axis=0, concat_axis=0, tiled=True),
        lax.all_to_all(send_value, "head", split_axis=0, concat_axis=0, tiled=True),
        lax.all_to_all(filled, "head", split_axis=0, concat_axis=0, tiled=True),
    )
    prepared = []
    lse_list = []
    head_outs = []
    for head_slot in range(local_heads):
        live_rows = recv_fill[:, head_slot].reshape(-1) > 0
        gather_order, landing, used_blocks = arrange(live_rows, BLOCK)
        live_use = live_rows
        pieces = (
            pick_rows(recv_query, head_slot),
            pick_rows(recv_key, head_slot),
            pick_rows(recv_value, head_slot),
        )
        pieces, live_use, gather_order, landing, used_blocks = (
            pieces,
            live_use,
            gather_order,
            landing,
            used_blocks,
        )
        row_lse, head_out = forward_head(
            pieces[0], pieces[1], pieces[2], live_use, sink_logits[head_slot], used_blocks, BLOCK
        )
        prepared.append((pieces, live_use, gather_order, landing, used_blocks))
        lse_list.append(row_lse)
        head_outs.append(head_out)
        out_list.append(restore(head_out, devices))
    back_out = lax.all_to_all(
        jnp.stack(out_list, axis=1), "head", split_axis=0, concat_axis=0, tiled=True
    )
    recv_cot = lax.all_to_all(send_cot, "head", split_axis=0, concat_axis=0, tiled=True)
    for head_slot in range(local_heads):
        pieces, live_use, gather_order, landing, used_blocks = prepared[head_slot]
        cot_rows = pick_rows(recv_cot, head_slot)
        qgrad, kgrad, vgrad, sink_term = backward_head(
            pieces[0],
            pieces[1],
            pieces[2],
            cot_rows,
            head_outs[head_slot],
            lse_list[head_slot],
            live_use,
            sink_logits[head_slot],
            used_blocks,
            BLOCK,
        )
        qgrad_list.append(restore(qgrad, devices))
        kgrad_list.append(restore(kgrad, devices))
        vgrad_list.append(restore(vgrad, devices))
        sink_list.append(sink_term)
    back_qgrad, back_kgrad, back_vgrad = (
        lax.all_to_all(
            jnp.stack(qgrad_list, axis=1), "head", split_axis=0, concat_axis=0, tiled=True
        ),
        lax.all_to_all(
            jnp.stack(kgrad_list, axis=1), "head", split_axis=0, concat_axis=0, tiled=True
        ),
        lax.all_to_all(
            jnp.stack(vgrad_list, axis=1), "head", split_axis=0, concat_axis=0, tiled=True
        ),
    )
    sink_grad = lax.psum(jnp.stack(sink_list), "dp")
    token_out = collect(back_out).astype(jnp.float32)
    mixed = (gate_probs[:, :, None] * token_out).astype(jnp.bfloat16)
    gate_sum = jnp.sum(out_grad[0].astype(jnp.float32) * token_out, axis=-1)
    gate_grad = gate_probs * (gate_sum - jnp.sum(gate_probs * gate_sum, axis=-1, keepdims=True))
    return (
        mixed[None],
        collect(back_qgrad)[None],
        collect(back_kgrad)[None],
        collect(back_vgrad)[None],
        gate_grad[None],
        sink_grad,
    )


def solution(mesh):
    placed = (
        P("dp", "head", None),
        P("dp", "head", None, None),
        P("dp", "head", None, None),
        P("dp", "head", None, None),
        P("dp", "head", None),
        P("head"),
        P("dp", "head", None, None),
    )
    return jax.shard_map(
        per_device,
        mesh=mesh,
        in_specs=placed,
        out_specs=(
            P("dp", "head", None, None),
            P("dp", "head", None, None),
            P("dp", "head", None, None),
            P("dp", "head", None, None),
            P("dp", "head", None),
            P("head"),
        ),
        check_vma=False,
    )
```

profile of v0, /device:TPU:0, one launch (start us, length us, event | category | flops | bytes accessed | tf_op | source)
XLA Modules:
  0.0 204.0 jit_solution(5614113830701706993)
XLA Ops:
  0.7 0.8 broadcast_multiply_fusion
  2.3 7.6 %scatter_custom_fusion = bf16[2048]{0:T(1024)(128)(2,1)S(1)} fusion(s32[1024]{0:T(1024)S(1)} %bitcast.236, bf16[1024]{0:T(1024)(128)(2,1)S(1)} %broadcast.376, bf16[]{:T(256)} %constant.402.clone.1), kind=kCustom, calls=%fused_computation.130 | custom fusion | bytes 4098 | tf_op jit(solution)/shard_map/scatter | solution.py:208
  10.6 7.4 %all-to-all-start = ((bf16[16,4,32]{2,1,0:T(4,128)(2,1)}), bf16[16,4,32]{2,1,0:T(4,128)(2,1)S(1)}, u32[]{:S(2)}, u32[]{:S(2)}) async-start(bf16[16,4,32]{2,1,0:T(4,128)(2,1)} %reshape.293), calls=%async_computation | async-start | bytes 32768 | tf_op jit(solution)/shard_map/all_to_all | solution.py:216
  18.0 4.0 %scatter_custom_fusion.2 = bf16[2048,128]{1,0:T(8,128)(2,1)} fusion(s32[1024]{0:T(1024)S(1)} %bitcast.237, bf16[1,128,8,128]{3,2,1,0:T(8,128)(2,1)S(1)} %copy-done, bf16[]{:T(256)} %constant.402.clone.1), kind=kCustom, calls=%fused_computation.91 | custom fusion | bytes 786434 | tf_op jit(solution)/shard_map/scatter | solution.py:190
  22.0 2.5 %all-to-all-done = bf16[16,4,32]{2,1,0:T(4,128)(2,1)S(1)} async-done(((bf16[16,4,32]{2,1,0:T(4,128)(2,1)}), bf16[16,4,32]{2,1,0:T(4,128)(2,1)S(1)}, u32[]{:S(2)}, u32[]{:S(2)}) %all-to-all-start) | async-done | bytes 4128 | tf_op jit(solution)/shard_map/all_to_all | solution.py:216
  24.5 3.7 %all-to-all-start.2 = ((bf16[16,4,32,128]{3,2,1,0:T(8,128)(2,1)}), bf16[16,4,32,128]{3,2,1,0:T(8,128)(2,1)S(1)}, u32[]{:S(2)}, u32[]{:S(2)}) async-start(bf16[16,4,32,128]{3,2,1,0:T(8,128)(2,1)} %bitcast.7), calls=%async_computation.2 | async-start | bytes 1048576 | tf_op jit(solution)/shard_map/all_to_all | solution.py:214
  28.2 4.0 %scatter_custom_fusion.1 = bf16[2048,128]{1,0:T(8,128)(2,1)} fusion(s32[1024]{0:T(1024)S(1)} %bitcast.238, bf16[1,128,8,128]{3,2,1,0:T(8,128)(2,1)S(1)} %copy-done.18, bf16[]{:T(256)} %constant.402.clone.1), kind=kCustom, calls=%fused_computation.93 | custom fusion | bytes 786434 | tf_op jit(solution)/shard_map/scatter | solution.py:190
  32.2 10.2 %all-to-all-done.2 = bf16[16,4,32,128]{3,2,1,0:T(8,128)(2,1)S(1)} async-done(((bf16[16,4,32,128]{3,2,1,0:T(8,128)(2,1)}), bf16[16,4,32,128]{3,2,1,0:T(8,128)(2,1)S(1)}, u32[]{:S(2)}, u32[]{:S(2)}) %all-to-all-start.2) | async-done | bytes 524320 | tf_op jit(solution)/shard_map/all_to_all | solution.py:214
  42.4 4.3 %all-to-all-start.1 = ((bf16[16,4,32,128]{3,2,1,0:T(8,128)(2,1)}), bf16[16,4,32,128]{3,2,1,0:T(8,128)(2,1)S(1)}, u32[]{:S(2)}, u32[]{:S(2)}) async-start(bf16[16,4,32,128]{3,2,1,0:T(8,128)(2,1)} %bitcast.4), calls=%async_computation.1 | async-start | bytes 1048576 | tf_op jit(solution)/shard_map/all_to_all | solution.py:213
  47.6 4.5 %scatter_custom_fusion.4 = bf16[2048,128]{1,0:T(8,128)(2,1)} fusion(s32[1024]{0:T(1024)S(1)} %bitcast.239, bf16[1,128,8,128]{3,2,1,0:T(8,128)(2,1)S(1)} %copy-done.4, f32[1024]{0:T(1024)S(1)} %exponential_divide_fusion, bf16[]{:T(256)} %constant.402.clone.1), kind=kCustom, calls=%fused_computation.88 | custom fusion | flops 393216 | bytes 790530 | tf_op jit(solution)/shard_map/scatter | solution.py:190
  52.1 8.8 %all-to-all-done.1 = bf16[16,4,32,128]{3,2,1,0:T(8,128)(2,1)S(1)} async-done(((bf16[16,4,32,128]{3,2,1,0:T(8,128)(2,1)}), bf16[16,4,32,128]{3,2,1,0:T(8,128)(2,1)S(1)}, u32[]{:S(2)}, u32[]{:S(2)}) %all-to-all-start.1) | async-done | bytes 524320 | tf_op jit(solution)/shard_map/all_to_all | solution.py:213
  61.0 4.3 %all-to-all-start.5 = ((bf16[16,4,32,128]{3,2,1,0:T(8,128)(2,1)}), bf16[16,4,32,128]{3,2,1,0:T(8,128)(2,1)S(1)}, u32[]{:S(2)}, u32[]{:S(2)}) async-start(bf16[16,4,32,128]{3,2,1,0:T(8,128)(2,1)} %bitcast.36), calls=%async_computation.5 | async-start | bytes 1048576 | tf_op jit(solution)/shard_map/all_to_all | solution.py:247
  65.3 4.0 %scatter_custom_fusion.3 = bf16[2048,128]{1,0:T(8,128)(2,1)} fusion(s32[1024]{0:T(1024)S(1)} %bitcast.240, bf16[1,128,8,128]{3,2,1,0:T(8,128)(2,1)S(1)} %copy-done.19, bf16[]{:T(256)} %constant.402.clone.1), kind=kCustom, calls=%fused_computation.89 | custom fusion | bytes 786434 | tf_op jit(solution)/shard_map/scatter | solution.py:190
  71.1 0.8 fusion.64
  72.3 7.3 %all-to-all-done.5 = bf16[16,4,32,128]{3,2,1,0:T(8,128)(2,1)S(1)} async-done(((bf16[16,4,32,128]{3,2,1,0:T(8,128)(2,1)}), bf16[16,4,32,128]{3,2,1,0:T(8,128)(2,1)S(1)}, u32[]{:S(2)}, u32[]{:S(2)}) %all-to-all-start.5) | async-done | bytes 524320 | tf_op jit(solution)/shard_map/all_to_all | solution.py:247
  79.5 4.2 %all-to-all-start.3 = ((bf16[16,4,32,128]{3,2,1,0:T(8,128)(2,1)}), bf16[16,4,32,128]{3,2,1,0:T(8,128)(2,1)S(1)}, u32[]{:S(2)}, u32[]{:S(2)}) async-start(bf16[16,4,32,128]{3,2,1,0:T(8,128)(2,1)} %bitcast.11), calls=%async_computation.3 | async-start | bytes 1048576 | tf_op jit(solution)/shard_map/all_to_all | solution.py:215
  86.2 11.8 %all-to-all-done.3 = bf16[16,4,32,128]{3,2,1,0:T(8,128)(2,1)S(1)} async-done(((bf16[16,4,32,128]{3,2,1,0:T(8,128)(2,1)}), bf16[16,4,32,128]{3,2,1,0:T(8,128)(2,1)S(1)}, u32[]{:S(2)}, u32[]{:S(2)}) %all-to-all-start.3) | async-done | bytes 524320 | tf_op jit(solution)/shard_map/all_to_all | solution.py:215
  98.7 1.1 multiply_reduce_fusion
  100.1 0.9 fusion.15
  103.4 1.1 multiply_reduce_fusion.3
  104.5 1.3 fusion.7
  105.8 0.9 fusion.12
  109.1 1.1 multiply_reduce_fusion.1
  113.5 0.9 pad_maximum_fusion.3
  114.4 4.2 %all-to-all-start.8 = ((bf16[16,4,32,128]{3,2,1,0:T(8,128)(2,1)}), bf16[16,4,32,128]{3,2,1,0:T(8,128)(2,1)S(1)}, u32[]{:S(2)}, u32[]{:S(2)}) async-start(bf16[16,4,32,128]{3,2,1,0:T(8,128)(2,1)} %pad_maximum_fusion.3), calls=%async_computation.8 | async-start | bytes 1048576 | tf_op jit(solution)/shard_map/all_to_all | solution.py:274
  118.6 1.2 fusion.14
  119.9 1.1 multiply_reduce_fusion.2
  121.0 1.6 fusion.6
  123.8 0.9 pad_maximum_fusion.2
  124.7 8.2 %all-to-all-done.8 = bf16[16,4,32,128]{3,2,1,0:T(8,128)(2,1)S(1)} async-done(((bf16[16,4,32,128]{3,2,1,0:T(8,128)(2,1)}), bf16[16,4,32,128]{3,2,1,0:T(8,128)(2,1)S(1)}, u32[]{:S(2)}, u32[]{:S(2)}) %all-to-all-start.8) | async-done | bytes 524320 | tf_op jit(solution)/shard_map/all_to_all | solution.py:274
  132.9 4.2 %all-to-all-start.7 = ((bf16[16,4,32,128]{3,2,1,0:T(8,128)(2,1)}), bf16[16,4,32,128]{3,2,1,0:T(8,128)(2,1)S(1)}, u32[]{:S(2)}, u32[]{:S(2)}) async-start(bf16[16,4,32,128]{3,2,1,0:T(8,128)(2,1)} %pad_maximum_fusion.2), calls=%async_computation.7 | async-start | bytes 1048576 | tf_op jit(solution)/shard_map/all_to_all | solution.py:271
  137.1 0.9 pad_maximum_fusion
  138.0 13.4 %all-to-all-done.7 = bf16[16,4,32,128]{3,2,1,0:T(8,128)(2,1)S(1)} async-done(((bf16[16,4,32,128]{3,2,1,0:T(8,128)(2,1)}), bf16[16,4,32,128]{3,2,1,0:T(8,128)(2,1)S(1)}, u32[]{:S(2)}, u32[]{:S(2)}) %all-to-all-start.7) | async-done | bytes 524320 | tf_op jit(solution)/shard_map/all_to_all | solution.py:271
  151.3 4.2 %all-to-all-start.4 = ((bf16[16,4,32,128]{3,2,1,0:T(8,128)(2,1)}), bf16[16,4,32,128]{3,2,1,0:T(8,128)(2,1)S(1)}, u32[]{:S(2)}, u32[]{:S(2)}) async-start(bf16[16,4,32,128]{3,2,1,0:T(8,128)(2,1)} %pad_maximum_fusion), calls=%async_computation.4 | async-start | bytes 1048576 | tf_op jit(solution)/shard_map/all_to_all | solution.py:244
  155.5 1.3 fusion.11
  156.8 1.2 multiply_reduce_fusion.5
  160.3 0.9 pad_maximum_fusion.1
  161.1 8.6 %all-to-all-done.4 = bf16[16,4,32,128]{3,2,1,0:T(8,128)(2,1)S(1)} async-done(((bf16[16,4,32,128]{3,2,1,0:T(8,128)(2,1)}), bf16[16,4,32,128]{3,2,1,0:T(8,128)(2,1)S(1)}, u32[]{:S(2)}, u32[]{:S(2)}) %all-to-all-start.4) | async-done | bytes 524320 | tf_op jit(solution)/shard_map/all_to_all | solution.py:244
  169.8 4.2 %all-to-all-start.6 = ((bf16[16,4,32,128]{3,2,1,0:T(8,128)(2,1)}), bf16[16,4,32,128]{3,2,1,0:T(8,128)(2,1)S(1)}, u32[]{:S(2)}, u32[]{:S(2)}) async-start(bf16[16,4,32,128]{3,2,1,0:T(8,128)(2,1)} %pad_maximum_fusion.1), calls=%async_computation.6 | async-start | bytes 1048576 | tf_op jit(solution)/shard_map/all_to_all | solution.py:268
  173.9 1.3 multiply_reduce_fusion.8
  176.5 1.3 multiply_reduce_fusion.6
  178.4 1.3 multiply_reduce_fusion.7
  180.4 5.4 %psum.7 = f32[4]{0:T(128)} all-reduce(f32[4]{0:T(128)S(1)} %pad_maximum_fusion.4), channel_id=1, replica_groups=mesh['dp'=2,'head'=16] {'dp'}, use_global_device_ids=true, to_apply=%region_28.29 | all-reduce | flops 4 | bytes 32 | tf_op jit(solution)/shard_map/psum | solution.py:278
  185.8 4.3 %gather_fusion.3 = bf16[1024,128]{1,0:T(8,128)(2,1)} fusion(bf16[2048,128]{1,0:T(8,128)(2,1)S(1)} %bitcast.179, s32[1024]{0:T(1024)S(1)} %broadcast_clamp_fusion), kind=kCustom, calls=%fused_computation.3 | custom fusion | bytes 528384 | tf_op jit(solution)/shard_map/gather | solution.py:195
  190.1 4.3 %gather_fusion.2 = bf16[1024,128]{1,0:T(8,128)(2,1)} fusion(bf16[2048,128]{1,0:T(8,128)(2,1)S(1)} %bitcast.180, s32[1024]{0:T(1024)S(1)} %broadcast_clamp_fusion), kind=kCustom, calls=%fused_computation.2 | custom fusion | bytes 528384 | tf_op jit(solution)/shard_map/gather | solution.py:195
  194.4 3.2 %gather_fusion = bf16[1024,128]{1,0:T(8,128)(2,1)S(1)} fusion(bf16[2048,128]{1,0:T(8,128)(2,1)S(1)} %bitcast.181, s32[1024]{0:T(1024)S(1)} %broadcast_clamp_fusion), kind=kCustom, calls=%fused_computation | custom fusion | bytes 528384 | tf_op jit(solution)/shard_map/gather | solution.py:195
  198.1 4.3 %gather_fusion.1 = bf16[1024,128]{1,0:T(8,128)(2,1)} fusion(bf16[2048,128]{1,0:T(8,128)(2,1)S(1)} %bitcast.182, s32[1024]{0:T(1024)S(1)} %broadcast_clamp_fusion), kind=kCustom, calls=%fused_computation.1 | custom fusion | bytes 528384 | tf_op jit(solution)/shard_map/gather | solution.py:195
  202.5 0.9 fusion.25
  (126 shorter events, 20.8 us)
Async XLA Ops:
  0.6 17.3 %copy-start = (bf16[1,128,8,128]{3,2,1,0:T(8,128)(2,1)S(1)}, bf16[1,128,8,128]{3,2,1,0:T(8,128)(2,1)}, u32[]{:S(2)}) copy-start(bf16[1,128,8,128]{3,2,1,0:T(8,128)(2,1)} %param.9) | copy-start | bytes 786436
  0.6 0.8 copy-start.29
  10.6 13.9 %all-to-all-start = ((bf16[16,4,32]{2,1,0:T(4,128)(2,1)}), bf16[16,4,32]{2,1,0:T(4,128)(2,1)S(1)}, u32[]{:S(2)}, u32[]{:S(2)}) async-start(bf16[16,4,32]{2,1,0:T(4,128)(2,1)} %reshape.293), calls=%async_computation | async-start | bytes 32768 | tf_op jit(solution)/shard_map/all_to_all | solution.py:216
  24.5 3.7 %copy-start.18 = (bf16[1,128,8,128]{3,2,1,0:T(8,128)(2,1)S(1)}, bf16[1,128,8,128]{3,2,1,0:T(8,128)(2,1)}, u32[]{:S(2)}) copy-start(bf16[1,128,8,128]{3,2,1,0:T(8,128)(2,1)} %param.8) | copy-start | bytes 786436
  24.5 17.9 %all-to-all-start.2 = ((bf16[16,4,32,128]{3,2,1,0:T(8,128)(2,1)}), bf16[16,4,32,128]{3,2,1,0:T(8,128)(2,1)S(1)}, u32[]{:S(2)}, u32[]{:S(2)}) async-start(bf16[16,4,32,128]{3,2,1,0:T(8,128)(2,1)} %bitcast.7), calls=%async_computation.2 | async-start | bytes 1048576 | tf_op jit(solution)/shard_map/all_to_all | solution.py:214
  42.4 4.3 %copy-start.28 = (f32[1,128,8]{1,2,0:T(8,128)S(1)}, f32[1,128,8]{1,2,0:T(8,128)}, u32[]{:S(2)}) copy-start(f32[1,128,8]{1,2,0:T(8,128)} %param.11) | copy-start | bytes 12292
  42.4 18.5 %all-to-all-start.1 = ((bf16[16,4,32,128]{3,2,1,0:T(8,128)(2,1)}), bf16[16,4,32,128]{3,2,1,0:T(8,128)(2,1)S(1)}, u32[]{:S(2)}, u32[]{:S(2)}) async-start(bf16[16,4,32,128]{3,2,1,0:T(8,128)(2,1)} %bitcast.4), calls=%async_computation.1 | async-start | bytes 1048576 | tf_op jit(solution)/shard_map/all_to_all | solution.py:213
  46.7 1.0 copy-start.4
  61.0 4.3 %copy-start.19 = (bf16[1,128,8,128]{3,2,1,0:T(8,128)(2,1)S(1)}, bf16[1,128,8,128]{3,2,1,0:T(8,128)(2,1)}, u32[]{:S(2)}) copy-start(bf16[1,128,8,128]{3,2,1,0:T(8,128)(2,1)} %param.10) | copy-start | bytes 786436
  61.0 18.6 %all-to-all-start.5 = ((bf16[16,4,32,128]{3,2,1,0:T(8,128)(2,1)}), bf16[16,4,32,128]{3,2,1,0:T(8,128)(2,1)S(1)}, u32[]{:S(2)}, u32[]{:S(2)}) async-start(bf16[16,4,32,128]{3,2,1,0:T(8,128)(2,1)} %bitcast.36), calls=%async_computation.5 | async-start | bytes 1048576 | tf_op jit(solution)/shard_map/all_to_all | solution.py:247
  65.3 4.0 %copy-start.30 = (f32[4]{0:T(128)S(1)}, f32[4]{0:T(128)}, u32[]{:S(2)}) copy-start(f32[4]{0:T(128)} %param.12) | copy-start | bytes 52
  71.1 0.8 copy-start.12
  71.1 30.0 %copy-start.10 = (bf16[16,1,32,128]{3,2,1,0:T(8,128)(2,1)}, bf16[16,1,32,128]{3,2,1,0:T(8,128)(2,1)S(1)}, u32[]{:S(2)}) copy-start(bf16[16,1,32,128]{3,2,1,0:T(8,128)(2,1)S(1)} %get-tuple-element.1312) | copy-start | bytes 393220
  71.1 35.6 %copy-start.8 = (bf16[16,1,32,128]{3,2,1,0:T(8,128)(2,1)}, bf16[16,1,32,128]{3,2,1,0:T(8,128)(2,1)S(1)}, u32[]{:S(2)}) copy-start(bf16[16,1,32,128]{3,2,1,0:T(8,128)(2,1)S(1)} %get-tuple-element.1314) | copy-start | bytes 393220
  71.9 34.8 %copy-start.15 = (bf16[16,1,32,128]{3,2,1,0:T(8,128)(2,1)}, bf16[16,1,32,128]{3,2,1,0:T(8,128)(2,1)S(1)}, u32[]{:S(2)}) copy-start(bf16[16,1,32,128]{3,2,1,0:T(8,128)(2,1)S(1)} %get-tuple-element.1318) | copy-start | bytes 393220
  79.5 18.4 %all-to-all-start.3 = ((bf16[16,4,32,128]{3,2,1,0:T(8,128)(2,1)}), bf16[16,4,32,128]{3,2,1,0:T(8,128)(2,1)S(1)}, u32[]{:S(2)}, u32[]{:S(2)}) async-start(bf16[16,4,32,128]{3,2,1,0:T(8,128)(2,1)} %bitcast.11), calls=%async_computation.3 | async-start | bytes 1048576 | tf_op jit(solution)/shard_map/all_to_all | solution.py:215
  85.9 17.6 %copy-start.26 = (bf16[16,1,32,128]{3,2,1,0:T(8,128)(2,1)}, bf16[16,1,32,128]{3,2,1,0:T(8,128)(2,1)S(1)}, u32[]{:S(2)}) copy-start(bf16[16,1,32,128]{3,2,1,0:T(8,128)(2,1)S(1)} %get-tuple-element.1308) | copy-start | bytes 393220
  110.2 0.9 copy-start.6
  110.2 1.0 copy-start.13
  111.5 8.4 %copy-start.3 = (f32[512,512]{0,1:T(8,128)}, f32[512,512]{0,1:T(8,128)S(1)}, u32[]{:S(2)}) copy-start(f32[512,512]{0,1:T(8,128)S(1)} %get-tuple-element.1333) | copy-start | bytes 3145732
  112.2 1.0 copy-start.21
  114.4 18.4 %all-to-all-start.8 = ((bf16[16,4,32,128]{3,2,1,0:T(8,128)(2,1)}), bf16[16,4,32,128]{3,2,1,0:T(8,128)(2,1)S(1)}, u32[]{:S(2)}, u32[]{:S(2)}) async-start(bf16[16,4,32,128]{3,2,1,0:T(8,128)(2,1)} %pad_maximum_fusion.3), calls=%async_computation.8 | async-start | bytes 1048576 | tf_op jit(solution)/shard_map/all_to_all | solution.py:274
  118.6 1.3 copy-start.22
  118.6 1.3 copy-start.24
  121.0 1.6 copy-start.14
  122.6 2.0 %copy-start.1 = (bf16[512,512]{0,1:T(8,128)(2,1)}, bf16[512,512]{0,1:T(8,128)(2,1)S(1)}, u32[]{:S(2)}) copy-start(bf16[512,512]{0,1:T(8,128)(2,1)S(1)} %fusion.6) | copy-start | bytes 1572868
  122.7 1.0 copy-start.16
  122.7 1.1 copy-start.17
  124.7 12.4 %copy-start.20 = (bf16[512,128]{1,0:T(8,128)(2,1)S(1)}, bf16[512,128]{1,0:T(8,128)(2,1)}, u32[]{:S(2)}) copy-start(bf16[512,128]{1,0:T(8,128)(2,1)} %get-tuple-element.1337) | copy-start | bytes 393220
  124.7 12.4 %copy-start.23 = (bf16[512,128]{1,0:T(8,128)(2,1)S(1)}, bf16[512,128]{1,0:T(8,128)(2,1)}, u32[]{:S(2)}) copy-start(bf16[512,128]{1,0:T(8,128)(2,1)} %get-tuple-element.1343) | copy-start | bytes 393220
  124.7 12.4 %copy-start.25 = (bf16[512,128]{1,0:T(8,128)(2,1)S(1)}, bf16[512,128]{1,0:T(8,128)(2,1)}, u32[]{:S(2)}) copy-start(bf16[512,128]{1,0:T(8,128)(2,1)} %get-tuple-element.1339) | copy-start | bytes 393220
  124.7 12.4 %copy-start.27 = (bf16[512,128]{1,0:T(8,128)(2,1)S(1)}, bf16[512,128]{1,0:T(8,128)(2,1)}, u32[]{:S(2)}) copy-start(bf16[512,128]{1,0:T(8,128)(2,1)} %get-tuple-element.1341) | copy-start | bytes 393220
  132.9 18.4 %all-to-all-start.7 = ((bf16[16,4,32,128]{3,2,1,0:T(8,128)(2,1)}), bf16[16,4,32,128]{3,2,1,0:T(8,128)(2,1)S(1)}, u32[]{:S(2)}, u32[]{:S(2)}) async-start(bf16[16,4,32,128]{3,2,1,0:T(8,128)(2,1)} %pad_maximum_fusion.2), calls=%async_computation.7 | async-start | bytes 1048576 | tf_op jit(solution)/shard_map/all_to_all | solution.py:271
  151.3 18.4 %all-to-all-start.4 = ((bf16[16,4,32,128]{3,2,1,0:T(8,128)(2,1)}), bf16[16,4,32,128]{3,2,1,0:T(8,128)(2,1)S(1)}, u32[]{:S(2)}, u32[]{:S(2)}) async-start(bf16[16,4,32,128]{3,2,1,0:T(8,128)(2,1)} %pad_maximum_fusion), calls=%async_computation.4 | async-start | bytes 1048576 | tf_op jit(solution)/shard_map/all_to_all | solution.py:244
  155.5 2.5 %copy-start.11 = (bf16[16,1,32,128]{3,2,1,0:T(8,128)(2,1)S(1)}, bf16[16,1,32,128]{3,2,1,0:T(8,128)(2,1)}, u32[]{:S(2)}) copy-start(bf16[16,1,32,128]{3,2,1,0:T(8,128)(2,1)} %copy-done.10) | copy-start | bytes 393220
  158.0 0.9 copy-start.9
  158.9 1.0 copy-start.2
  158.9 1.1 copy-start.7
  169.8 28.4 %all-to-all-start.6 = ((bf16[16,4,32,128]{3,2,1,0:T(8,128)(2,1)}), bf16[16,4,32,128]{3,2,1,0:T(8,128)(2,1)S(1)}, u32[]{:S(2)}, u32[]{:S(2)}) async-start(bf16[16,4,32,128]{3,2,1,0:T(8,128)(2,1)} %pad_maximum_fusion.1), calls=%async_computation.6 | async-start | bytes 1048576 | tf_op jit(solution)/shard_map/all_to_all | solution.py:268
  194.4 3.2 %copy-start.5 = (bf16[1,128,8,128]{3,2,1,0:T(8,128)(2,1)S(1)}, bf16[1,128,8,128]{3,2,1,0:T(8,128)(2,1)}, u32[]{:S(2)}) copy-start(bf16[1,128,8,128]{3,2,1,0:T(8,128)(2,1)} %param.13) | copy-start | bytes 786436
where the time goes:
time: 205 us; the launch traced here: 204 us
  waiting for transfers between devices  70.8 us (35%)
  local copies, waits for them, and re-layouts  44.4 us (22%)
  starting transfers between devices  40.5 us (20%)
  other arithmetic  22.6 us (11%)
  matrix products  16.5 us (8%)
  blocking collectives  5.42 us (3%)
  between operations  3.8 us (2%)
    gather x4, local copies, waits for them, and re-layouts, collect(): buffer.reshape(buffer_rows, buffer.shape[-1])[target]  16.1 us
    all_to_all x1, waiting for transfers between devices, per_device(): lax.all_to_all(jnp.stack(kgrad_list, axis=1), 'head', split_axis=0, conca...  13.4 us
    scatter x3, local copies, waits for them, and re-layouts, spread_out(): jnp.zeros((buffer_rows, flat_rows.shape[-1]), flat_rows.dtype).at[target]  12 us
    all_to_all x1, waiting for transfers between devices, per_device(): lax.all_to_all(send_value, 'head', split_axis=0, concat_axis=0, tiled=True)  11.8 us
    all_to_all x1, waiting for transfers between devices, per_device(): lax.all_to_all(send_key, 'head', split_axis=0, concat_axis=0, tiled=True)  10.2 us
    all_to_all x1, waiting for transfers between devices, per_device(): lax.all_to_all(send_query, 'head', split_axis=0, concat_axis=0, tiled=True)  8.84 us
    all_to_all x1, waiting for transfers between devices, per_device(): lax.all_to_all(jnp.stack(out_list, axis=1), 'head', split_axis=0, concat_...  8.62 us
    all_to_all x1, waiting for transfers between devices, per_device(): lax.all_to_all(jnp.stack(vgrad_list, axis=1), 'head', split_axis=0, conca...  8.16 us
  transfers between devices with their start and end apart: 9, of which 8 were waited for; matrix products, arithmetic and copies ran while one was open for 24% of the time, Pallas kernels for 0%

commit v1 on v0

--- a/solution.py
+++ b/solution.py
@@ -244,7 +244,19 @@
     back_out = lax.all_to_all(
         jnp.stack(out_list, axis=1), "head", split_axis=0, concat_axis=0, tiled=True
     )
-    recv_cot = lax.all_to_all(send_cot, "head", split_axis=0, concat_axis=0, tiled=True)
+    ways, here = (lax.axis_size("head"), lax.axis_index("head"))
+    width_2 = send_cot.shape[0] // ways
+    shape = list(send_cot.shape)
+    shape[0] = width_2
+    height = shape[0]
+    shape[0] = height * ways
+    full = jnp.zeros(shape, send_cot.dtype)
+    for mask in range(ways):
+        part = lax.dynamic_slice_in_dim(send_cot, (here ^ mask) * width_2, width_2, axis=0)
+        if mask:
+            part = lax.ppermute(part, "head", [(d, d ^ mask) for d in range(ways)])
+        full = lax.dynamic_update_slice_in_dim(full, part, (here ^ mask) * height, axis=0)
+    recv_cot = full
     for head_slot in range(local_heads):
         pieces, live_use, gather_order, landing, used_blocks = prepared[head_slot]
         cot_rows = pick_rows(recv_cot, head_slot)

time: 205 us -> 243 us (1.19)
  waiting for transfers between devices: 70.8 us -> 93.3 us
  starting transfers between devices: 40.5 us -> 53.8 us
    ppermute x0 -> x15, waiting for transfers between devices: none -> 39.7 us  [per_device(): part = lax.ppermute(part, 'head', [(d, d ^ mask) for d in range(ways)])]
    ppermute x0 -> x15, starting transfers between devices: none -> 15.9 us  [per_device(): part = lax.ppermute(part, 'head', [(d, d ^ mask) for d in range(ways)])]
    all_to_all x1, waiting for transfers between devices: 10.2 us -> 0.01 us  [per_device(): lax.all_to_all(send_key, 'head', split_axis=0, concat_axis=0, tiled=True)]
    all_to_all x1 -> x0, waiting for transfers between devices: 7.28 us -> none  [per_device(): lax.all_to_all(send_cot, 'head', split_axis=0, concat_axis=0, tiled=True)]
    all_to_all x1 -> x0, starting transfers between devices: 4.3 us -> none  [per_device(): lax.all_to_all(send_cot, 'head', split_axis=0, concat_axis=0, tiled=True)]
    all_to_all x1, waiting for transfers between devices: 8.84 us -> 12.8 us  [per_device(): lax.all_to_all(send_query, 'head', split_axis=0, concat_axis=0, tiled=True)]
    all_to_all x1, waiting for transfers between devices: 2.51 us -> 0.01 us  [per_device(): lax.all_to_all(filled, 'head', split_axis=0, concat_axis=0, tiled=True)]
  transfers between devices with their start and end apart: 9 -> 23, of which waited for: 8 -> 15; matrix products, arithmetic and copies ran while one was open for 24% -> 20% of each run, Pallas kernels for 0% -> 0%
where the time goes in v1:
time: 243 us; the launch traced here: 241 us
  waiting for transfers between devices  93.3 us (38%)
  starting transfers between devices  53.8 us (22%)
  local copies, waits for them, and re-layouts  46.4 us (19%)
  other arithmetic  22 us (9%)
  matrix products  16.3 us (7%)
  blocking collectives  5.42 us (2%)
  between operations  4.01 us (2%)
    ppermute x15, waiting for transfers between devices, per_device(): part = lax.ppermute(part, 'head', [(d, d ^ mask) for d in range(ways)])  39.7 us
    gather x4, local copies, waits for them, and re-layouts, collect(): buffer.reshape(buffer_rows, buffer.shape[-1])[target]  16.1 us
    ppermute x15, starting transfers between devices, per_device(): part = lax.ppermute(part, 'head', [(d, d ^ mask) for d in range(ways)])  15.9 us
    all_to_all x1, waiting for transfers between devices, per_device(): lax.all_to_all(jnp.stack(kgrad_list, axis=1), 'head', split_axis=0, conca...  13.4 us
    all_to_all x1, waiting for transfers between devices, per_device(): lax.all_to_all(send_query, 'head', split_axis=0, concat_axis=0, tiled=True)  12.8 us
    scatter x3, local copies, waits for them, and re-layouts, spread_out(): jnp.zeros((buffer_rows, flat_rows.shape[-1]), flat_rows.dtype).at[target]  12 us
    all_to_all x1, waiting for transfers between devices, per_device(): lax.all_to_all(send_value, 'head', split_axis=0, concat_axis=0, tiled=True)  10.8 us
    all_to_all x1, waiting for transfers between devices, per_device(): lax.all_to_all(jnp.stack(out_list, axis=1), 'head', split_axis=0, concat_...  8.63 us
  transfers between devices with their start and end apart: 23, of which 15 were waited for; matrix products, arithmetic and copies ran while one was open for 20% of the time, Pallas kernels for 0%

profile of v1, /device:TPU:0, one launch (start us, length us, event | category | flops | bytes accessed | tf_op | source)
XLA Modules:
  0.0 241.3 jit_solution(17973165538887102105)
XLA Ops:
  2.3 7.6 %scatter_custom_fusion = bf16[2048]{0:T(1024)(128)(2,1)S(1)} fusion(s32[1024]{0:T(1024)S(1)} %bitcast.270, bf16[1024]{0:T(1024)(128)(2,1)S(1)} %broadcast.376, bf16[]{:T(256)} %constant.422.clone.1), kind=kCustom, calls=%fused_computation.161 | custom fusion | bytes 4098 | tf_op jit(solution)/shard_map/scatter | solution.py:208
  10.6 7.4 %all-to-all-start = ((bf16[16,4,32]{2,1,0:T(4,128)(2,1)}), bf16[16,4,32]{2,1,0:T(4,128)(2,1)S(1)}, u32[]{:S(2)}, u32[]{:S(2)}) async-start(bf16[16,4,32]{2,1,0:T(4,128)(2,1)} %reshape.293), calls=%async_computation | async-start | bytes 32768 | tf_op jit(solution)/shard_map/all_to_all | solution.py:216
  19.7 3.8 %scatter_custom_fusion.4 = bf16[2048,128]{1,0:T(8,128)(2,1)S(1)} fusion(s32[1024]{0:T(1024)S(1)} %bitcast.271, bf16[1,128,8,128]{3,2,1,0:T(8,128)(2,1)S(1)} %copy-done.4, f32[1024]{0:T(1024)S(1)} %exponential_divide_fusion, bf16[]{:T(256)} %constant.422.clone.1), kind=kCustom, calls=%fused_computation.88 | custom fusion | flops 393216 | bytes 790530 | tf_op jit(solution)/shard_map/scatter | solution.py:190
  23.7 4.4 %collective-permute-start.14 = (bf16[1,4,32,128]{3,2,1,0:T(8,128)(2,1)S(1)}, bf16[1,4,32,128]{3,2,1,0:T(8,128)(2,1)S(1)}, u32[]{:S(2)}, u32[]{:S(2)}) collective-permute-start(bf16[1,4,32,128]{3,2,1,0:T(8,128)(2,1)S(1)} %get-tuple-element.1312), channel_id=1, source_target_pairs={{0,15},{1,14},{2,13},{3,12},{4,11},{5,10},{6,9},{7,8},{8,7},{9,6},... | collective-permute-start | bytes 98312 | tf_op jit(solution)/shard_map/ppermute | solution.py:257
  28.4 3.2 %collective-permute-start.12 = (bf16[1,4,32,128]{3,2,1,0:T(8,128)(2,1)S(1)}, bf16[1,4,32,128]{3,2,1,0:T(8,128)(2,1)S(1)}, u32[]{:S(2)}, u32[]{:S(2)}) collective-permute-start(bf16[1,4,32,128]{3,2,1,0:T(8,128)(2,1)S(1)} %get-tuple-element.1314), channel_id=1, source_target_pairs={{0,13},{1,12},{2,15},{3,14},{4,9},{5,8},{6,11},{7,10},{8,5},{9,4},... | collective-permute-start | bytes 98312 | tf_op jit(solution)/shard_map/ppermute | solution.py:257
  33.5 4.0 %scatter_custom_fusion.3 = bf16[2048,128]{1,0:T(8,128)(2,1)} fusion(s32[1024]{0:T(1024)S(1)} %bitcast.272, bf16[1,128,8,128]{3,2,1,0:T(8,128)(2,1)S(1)} %copy-done, bf16[]{:T(256)} %constant.422.clone.1), kind=kCustom, calls=%fused_computation.89 | custom fusion | bytes 786434 | tf_op jit(solution)/shard_map/scatter | solution.py:190
  37.4 4.0 %scatter_custom_fusion.2 = bf16[2048,128]{1,0:T(8,128)(2,1)} fusion(s32[1024]{0:T(1024)S(1)} %bitcast.273, bf16[1,128,8,128]{3,2,1,0:T(8,128)(2,1)S(1)} %copy-done.18, bf16[]{:T(256)} %constant.422.clone.1), kind=kCustom, calls=%fused_computation.91 | custom fusion | bytes 786434 | tf_op jit(solution)/shard_map/scatter | solution.py:190
  41.4 4.0 %scatter_custom_fusion.1 = bf16[2048,128]{1,0:T(8,128)(2,1)} fusion(s32[1024]{0:T(1024)S(1)} %bitcast.274, bf16[1,128,8,128]{3,2,1,0:T(8,128)(2,1)S(1)} %copy-done.19, bf16[]{:T(256)} %constant.422.clone.1), kind=kCustom, calls=%fused_computation.93 | custom fusion | bytes 786434 | tf_op jit(solution)/shard_map/scatter | solution.py:190
  45.4 5.7 %all-to-all-start.2 = ((bf16[16,4,32,128]{3,2,1,0:T(8,128)(2,1)}), bf16[16,4,32,128]{3,2,1,0:T(8,128)(2,1)S(1)}, u32[]{:S(2)}, u32[]{:S(2)}) async-start(bf16[16,4,32,128]{3,2,1,0:T(8,128)(2,1)} %bitcast.7), calls=%async_computation.2 | async-start | bytes 1048576 | tf_op jit(solution)/shard_map/all_to_all | solution.py:214
  51.6 1.9 collective-permute-start.1
  53.6 4.3 %collective-permute-done.1 = bf16[1,4,32,128]{3,2,1,0:T(8,128)(2,1)S(1)} collective-permute-done((bf16[1,4,32,128]{3,2,1,0:T(8,128)(2,1)S(1)}, bf16[1,4,32,128]{3,2,1,0:T(8,128)(2,1)S(1)}, u32[]{:S(2)}, u32[]{:S(2)}) %collective-permute-start.1) | collective-permute-done | bytes 32800 | tf_op jit(solution)/shard_map/ppermute | solution.py:257
  57.9 3.6 %collective-permute-done.2 = bf16[1,4,32,128]{3,2,1,0:T(8,128)(2,1)S(1)} collective-permute-done((bf16[1,4,32,128]{3,2,1,0:T(8,128)(2,1)S(1)}, bf16[1,4,32,128]{3,2,1,0:T(8,128)(2,1)S(1)}, u32[]{:S(2)}, u32[]{:S(2)}) %collective-permute-start.2) | collective-permute-done | bytes 32800 | tf_op jit(solution)/shard_map/ppermute | solution.py:257
  61.5 4.2 %collective-permute-done.3 = bf16[1,4,32,128]{3,2,1,0:T(8,128)(2,1)S(1)} collective-permute-done((bf16[1,4,32,128]{3,2,1,0:T(8,128)(2,1)S(1)}, bf16[1,4,32,128]{3,2,1,0:T(8,128)(2,1)S(1)}, u32[]{:S(2)}, u32[]{:S(2)}) %collective-permute-start.3) | collective-permute-done | bytes 32800 | tf_op jit(solution)/shard_map/ppermute | solution.py:257
  65.7 3.3 %collective-permute-done.4 = bf16[1,4,32,128]{3,2,1,0:T(8,128)(2,1)S(1)} collective-permute-done((bf16[1,4,32,128]{3,2,1,0:T(8,128)(2,1)S(1)}, bf16[1,4,32,128]{3,2,1,0:T(8,128)(2,1)S(1)}, u32[]{:S(2)}, u32[]{:S(2)}) %collective-permute-start.4) | collective-permute-done | bytes 32800 | tf_op jit(solution)/shard_map/ppermute | solution.py:257
  69.8 4.0 %collective-permute-done.5 = bf16[1,4,32,128]{3,2,1,0:T(8,128)(2,1)S(1)} collective-permute-done((bf16[1,4,32,128]{3,2,1,0:T(8,128)(2,1)S(1)}, bf16[1,4,32,128]{3,2,1,0:T(8,128)(2,1)S(1)}, u32[]{:S(2)}, u32[]{:S(2)}) %collective-permute-start.5) | collective-permute-done | bytes 32800 | tf_op jit(solution)/shard_map/ppermute | solution.py:257
  73.8 4.2 %collective-permute-done.6 = bf16[1,4,32,128]{3,2,1,0:T(8,128)(2,1)S(1)} collective-permute-done((bf16[1,4,32,128]{3,2,1,0:T(8,128)(2,1)S(1)}, bf16[1,4,32,128]{3,2,1,0:T(8,128)(2,1)S(1)}, u32[]{:S(2)}, u32[]{:S(2)}) %collective-permute-start.6) | collective-permute-done | bytes 32800 | tf_op jit(solution)/shard_map/ppermute | solution.py:257
  78.0 2.1 collective-permute-start.7
  80.1 2.7 %collective-permute-done.7 = bf16[1,4,32,128]{3,2,1,0:T(8,128)(2,1)S(1)} collective-permute-done((bf16[1,4,32,128]{3,2,1,0:T(8,128)(2,1)S(1)}, bf16[1,4,32,128]{3,2,1,0:T(8,128)(2,1)S(1)}, u32[]{:S(2)}, u32[]{:S(2)}) %collective-permute-start.7) | collective-permute-done | bytes 32800 | tf_op jit(solution)/shard_map/ppermute | solution.py:257
  82.9 4.3 %collective-permute-done.8 = bf16[1,4,32,128]{3,2,1,0:T(8,128)(2,1)S(1)} collective-permute-done((bf16[1,4,32,128]{3,2,1,0:T(8,128)(2,1)S(1)}, bf16[1,4,32,128]{3,2,1,0:T(8,128)(2,1)S(1)}, u32[]{:S(2)}, u32[]{:S(2)}) %collective-permute-start.8) | collective-permute-done | bytes 32800 | tf_op jit(solution)/shard_map/ppermute | solution.py:257
  87.2 2.6 %collective-permute-start.9 = (bf16[1,4,32,128]{3,2,1,0:T(8,128)(2,1)S(1)}, bf16[1,4,32,128]{3,2,1,0:T(8,128)(2,1)S(1)}, u32[]{:S(2)}, u32[]{:S(2)}) collective-permute-start(bf16[1,4,32,128]{3,2,1,0:T(8,128)(2,1)S(1)} %get-tuple-element.1317), channel_id=1, source_target_pairs={{0,10},{1,11},{2,8},{3,9},{4,14},{5,15},{6,12},{7,13},{8,2},{9,3},... | collective-permute-start | bytes 98312 | tf_op jit(solution)/shard_map/ppermute | solution.py:257
  89.8 3.7 %collective-permute-done.9 = bf16[1,4,32,128]{3,2,1,0:T(8,128)(2,1)S(1)} collective-permute-done((bf16[1,4,32,128]{3,2,1,0:T(8,128)(2,1)S(1)}, bf16[1,4,32,128]{3,2,1,0:T(8,128)(2,1)S(1)}, u32[]{:S(2)}, u32[]{:S(2)}) %collective-permute-start.9) | collective-permute-done | bytes 32800 | tf_op jit(solution)/shard_map/ppermute | solution.py:257
  93.6 5.3 %collective-permute-done.10 = bf16[1,4,32,128]{3,2,1,0:T(8,128)(2,1)S(1)} collective-permute-done((bf16[1,4,32,128]{3,2,1,0:T(8,128)(2,1)S(1)}, bf16[1,4,32,128]{3,2,1,0:T(8,128)(2,1)S(1)}, u32[]{:S(2)}, u32[]{:S(2)}) %collective-permute-start.10) | collective-permute-done | bytes 32800 | tf_op jit(solution)/shard_map/ppermute | solution.py:257
  99.0 4.0 %all-to-all-start.1 = ((bf16[16,4,32,128]{3,2,1,0:T(8,128)(2,1)}), bf16[16,4,32,128]{3,2,1,0:T(8,128)(2,1)S(1)}, u32[]{:S(2)}, u32[]{:S(2)}) async-start(bf16[16,4,32,128]{3,2,1,0:T(8,128)(2,1)} %bitcast.4), calls=%async_computation.1 | async-start | bytes 1048576 | tf_op jit(solution)/shard_map/all_to_all | solution.py:213
  104.4 12.8 %all-to-all-done.1 = bf16[16,4,32,128]{3,2,1,0:T(8,128)(2,1)S(1)} async-done(((bf16[16,4,32,128]{3,2,1,0:T(8,128)(2,1)}), bf16[16,4,32,128]{3,2,1,0:T(8,128)(2,1)S(1)}, u32[]{:S(2)}, u32[]{:S(2)}) %all-to-all-start.1) | async-done | bytes 524320 | tf_op jit(solution)/shard_map/all_to_all | solution.py:213
  117.2 4.2 %all-to-all-start.3 = ((bf16[16,4,32,128]{3,2,1,0:T(8,128)(2,1)}), bf16[16,4,32,128]{3,2,1,0:T(8,128)(2,1)S(1)}, u32[]{:S(2)}, u32[]{:S(2)}) async-start(bf16[16,4,32,128]{3,2,1,0:T(8,128)(2,1)} %bitcast.11), calls=%async_computation.3 | async-start | bytes 1048576 | tf_op jit(solution)/shard_map/all_to_all | solution.py:215
  124.9 10.8 %all-to-all-done.3 = bf16[16,4,32,128]{3,2,1,0:T(8,128)(2,1)S(1)} async-done(((bf16[16,4,32,128]{3,2,1,0:T(8,128)(2,1)}), bf16[16,4,32,128]{3,2,1,0:T(8,128)(2,1)S(1)}, u32[]{:S(2)}, u32[]{:S(2)}) %all-to-all-start.3) | async-done | bytes 524320 | tf_op jit(solution)/shard_map/all_to_all | solution.py:215
  136.4 1.1 multiply_reduce_fusion
  145.9 1.1 multiply_reduce_fusion.1
  151.7 4.2 %all-to-all-start.7 = ((bf16[16,4,32,128]{3,2,1,0:T(8,128)(2,1)}), bf16[16,4,32,128]{3,2,1,0:T(8,128)(2,1)S(1)}, u32[]{:S(2)}, u32[]{:S(2)}) async-start(bf16[16,4,32,128]{3,2,1,0:T(8,128)(2,1)} %pad_maximum_fusion.3), calls=%async_computation.7 | async-start | bytes 1048576 | tf_op jit(solution)/shard_map/all_to_all | solution.py:286
  155.9 1.2 fusion.14
  157.2 1.1 multiply_reduce_fusion.2
  158.3 1.6 fusion.6
  162.0 8.2 %all-to-all-done.7 = bf16[16,4,32,128]{3,2,1,0:T(8,128)(2,1)S(1)} async-done(((bf16[16,4,32,128]{3,2,1,0:T(8,128)(2,1)}), bf16[16,4,32,128]{3,2,1,0:T(8,128)(2,1)S(1)}, u32[]{:S(2)}, u32[]{:S(2)}) %all-to-all-start.7) | async-done | bytes 524320 | tf_op jit(solution)/shard_map/all_to_all | solution.py:286
  170.2 4.2 %all-to-all-start.6 = ((bf16[16,4,32,128]{3,2,1,0:T(8,128)(2,1)}), bf16[16,4,32,128]{3,2,1,0:T(8,128)(2,1)S(1)}, u32[]{:S(2)}, u32[]{:S(2)}) async-start(bf16[16,4,32,128]{3,2,1,0:T(8,128)(2,1)} %pad_maximum_fusion.2), calls=%async_computation.6 | async-start | bytes 1048576 | tf_op jit(solution)/shard_map/all_to_all | solution.py:283
  175.3 13.4 %all-to-all-done.6 = bf16[16,4,32,128]{3,2,1,0:T(8,128)(2,1)S(1)} async-done(((bf16[16,4,32,128]{3,2,1,0:T(8,128)(2,1)}), bf16[16,4,32,128]{3,2,1,0:T(8,128)(2,1)S(1)}, u32[]{:S(2)}, u32[]{:S(2)}) %all-to-all-start.6) | async-done | bytes 524320 | tf_op jit(solution)/shard_map/all_to_all | solution.py:283
  188.6 4.2 %all-to-all-start.4 = ((bf16[16,4,32,128]{3,2,1,0:T(8,128)(2,1)}), bf16[16,4,32,128]{3,2,1,0:T(8,128)(2,1)S(1)}, u32[]{:S(2)}, u32[]{:S(2)}) async-start(bf16[16,4,32,128]{3,2,1,0:T(8,128)(2,1)} %pad_maximum_fusion), calls=%async_computation.4 | async-start | bytes 1048576 | tf_op jit(solution)/shard_map/all_to_all | solution.py:244
  192.8 1.3 fusion.11
  194.1 1.2 multiply_reduce_fusion.5
  198.4 8.6 %all-to-all-done.4 = bf16[16,4,32,128]{3,2,1,0:T(8,128)(2,1)S(1)} async-done(((bf16[16,4,32,128]{3,2,1,0:T(8,128)(2,1)}), bf16[16,4,32,128]{3,2,1,0:T(8,128)(2,1)S(1)}, u32[]{:S(2)}, u32[]{:S(2)}) %all-to-all-start.4) | async-done | bytes 524320 | tf_op jit(solution)/shard_map/all_to_all | solution.py:244
  207.1 4.2 %all-to-all-start.5 = ((bf16[16,4,32,128]{3,2,1,0:T(8,128)(2,1)}), bf16[16,4,32,128]{3,2,1,0:T(8,128)(2,1)S(1)}, u32[]{:S(2)}, u32[]{:S(2)}) async-start(bf16[16,4,32,128]{3,2,1,0:T(8,128)(2,1)} %pad_maximum_fusion.1), calls=%async_computation.5 | async-start | bytes 1048576 | tf_op jit(solution)/shard_map/all_to_all | solution.py:280
  211.2 1.3 multiply_reduce_fusion.8
  213.8 1.3 multiply_reduce_fusion.6
  215.7 1.3 multiply_reduce_fusion.7
  217.7 5.4 %psum.7 = f32[4]{0:T(128)} all-reduce(f32[4]{0:T(128)S(1)} %pad_maximum_fusion.4), channel_id=1, replica_groups=mesh['dp'=2,'head'=16] {'dp'}, use_global_device_ids=true, to_apply=%region_28.29 | all-reduce | flops 4 | bytes 32 | tf_op jit(solution)/shard_map/psum | solution.py:290
  223.1 4.3 %gather_fusion.3 = bf16[1024,128]{1,0:T(8,128)(2,1)} fusion(bf16[2048,128]{1,0:T(8,128)(2,1)S(1)} %bitcast.211, s32[1024]{0:T(1024)S(1)} %broadcast_clamp_fusion), kind=kCustom, calls=%fused_computation.3 | custom fusion | bytes 528384 | tf_op jit(solution)/shard_map/gather | solution.py:195
  227.4 4.3 %gather_fusion.2 = bf16[1024,128]{1,0:T(8,128)(2,1)} fusion(bf16[2048,128]{1,0:T(8,128)(2,1)S(1)} %bitcast.212, s32[1024]{0:T(1024)S(1)} %broadcast_clamp_fusion), kind=kCustom, calls=%fused_computation.2 | custom fusion | bytes 528384 | tf_op jit(solution)/shard_map/gather | solution.py:195
  231.8 3.2 %gather_fusion = bf16[1024,128]{1,0:T(8,128)(2,1)S(1)} fusion(bf16[2048,128]{1,0:T(8,128)(2,1)S(1)} %bitcast.213, s32[1024]{0:T(1024)S(1)} %broadcast_clamp_fusion), kind=kCustom, calls=%fused_computation | custom fusion | bytes 528384 | tf_op jit(solution)/shard_map/gather | solution.py:195
  235.5 4.3 %gather_fusion.1 = bf16[1024,128]{1,0:T(8,128)(2,1)} fusion(bf16[2048,128]{1,0:T(8,128)(2,1)S(1)} %bitcast.214, s32[1024]{0:T(1024)S(1)} %broadcast_clamp_fusion), kind=kCustom, calls=%fused_computation.1 | custom fusion | bytes 528384 | tf_op jit(solution)/shard_map/gather | solution.py:195
  (172 shorter events, 34.6 us)
Async XLA Ops:
  0.6 32.8 %copy-start = (bf16[1,128,8,128]{3,2,1,0:T(8,128)(2,1)S(1)}, bf16[1,128,8,128]{3,2,1,0:T(8,128)(2,1)}, u32[]{:S(2)}) copy-start(bf16[1,128,8,128]{3,2,1,0:T(8,128)(2,1)} %param.10) | copy-start | bytes 786436
  10.6 34.9 %all-to-all-start = ((bf16[16,4,32]{2,1,0:T(4,128)(2,1)}), bf16[16,4,32]{2,1,0:T(4,128)(2,1)S(1)}, u32[]{:S(2)}, u32[]{:S(2)}) async-start(bf16[16,4,32]{2,1,0:T(4,128)(2,1)} %reshape.293), calls=%async_computation | async-start | bytes 32768 | tf_op jit(solution)/shard_map/all_to_all | solution.py:216
  18.7 0.9 copy-start.4
  23.7 79.3 %collective-permute-start.14 = (bf16[1,4,32,128]{3,2,1,0:T(8,128)(2,1)S(1)}, bf16[1,4,32,128]{3,2,1,0:T(8,128)(2,1)S(1)}, u32[]{:S(2)}, u32[]{:S(2)}) collective-permute-start(bf16[1,4,32,128]{3,2,1,0:T(8,128)(2,1)S(1)} %get-tuple-element.1312), channel_id=1, source_target_pairs={{0,15},{1,14},{2,13},{3,12},{4,11},{5,10},{6,9},{7,8},{8,7},{9,6},... | collective-permute-start | bytes 98312 | tf_op jit(solution)/shard_map/ppermute | solution.py:257
  28.0 75.0 %collective-permute-start.13 = (bf16[1,4,32,128]{3,2,1,0:T(8,128)(2,1)S(1)}, bf16[1,4,32,128]{3,2,1,0:T(8,128)(2,1)S(1)}, u32[]{:S(2)}, u32[]{:S(2)}) collective-permute-start(bf16[1,4,32,128]{3,2,1,0:T(8,128)(2,1)S(1)} %get-tuple-element.1313), channel_id=1, source_target_pairs={{0,14},{1,15},{2,12},{3,13},{4,10},{5,11},{6,8},{7,9},{8,6},{9,7},... | collective-permute-start | bytes 98312 | tf_op jit(solution)/shard_map/ppermute | solution.py:257
  28.4 74.5 %collective-permute-start.12 = (bf16[1,4,32,128]{3,2,1,0:T(8,128)(2,1)S(1)}, bf16[1,4,32,128]{3,2,1,0:T(8,128)(2,1)S(1)}, u32[]{:S(2)}, u32[]{:S(2)}) collective-permute-start(bf16[1,4,32,128]{3,2,1,0:T(8,128)(2,1)S(1)} %get-tuple-element.1314), channel_id=1, source_target_pairs={{0,13},{1,12},{2,15},{3,14},{4,9},{5,8},{6,11},{7,10},{8,5},{9,4},... | collective-permute-start | bytes 98312 | tf_op jit(solution)/shard_map/ppermute | solution.py:257
  31.6 67.4 %collective-permute-start.11 = (bf16[1,4,32,128]{3,2,1,0:T(8,128)(2,1)S(1)}, bf16[1,4,32,128]{3,2,1,0:T(8,128)(2,1)S(1)}, u32[]{:S(2)}, u32[]{:S(2)}) collective-permute-start(bf16[1,4,32,128]{3,2,1,0:T(8,128)(2,1)S(1)} %get-tuple-element.1315), channel_id=1, source_target_pairs={{0,12},{1,13},{2,14},{3,15},{4,8},{5,9},{6,10},{7,11},{8,4},{9,5},... | collective-permute-start | bytes 98312 | tf_op jit(solution)/shard_map/ppermute | solution.py:257
  31.8 19.8 %collective-permute-start = (bf16[1,4,32,128]{3,2,1,0:T(8,128)(2,1)S(1)}, bf16[1,4,32,128]{3,2,1,0:T(8,128)(2,1)S(1)}, u32[]{:S(2)}, u32[]{:S(2)}) collective-permute-start(bf16[1,4,32,128]{3,2,1,0:T(8,128)(2,1)S(1)} %get-tuple-element.1326), channel_id=1, source_target_pairs={{0,1},{1,0},{2,3},{3,2},{4,5},{5,4},{6,7},{7,6},{8,9},{9,8},{10,11... | collective-permute-start | bytes 98312 | tf_op jit(solution)/shard_map/ppermute | solution.py:257
  33.5 4.0 %copy-start.18 = (bf16[1,128,8,128]{3,2,1,0:T(8,128)(2,1)S(1)}, bf16[1,128,8,128]{3,2,1,0:T(8,128)(2,1)}, u32[]{:S(2)}) copy-start(bf16[1,128,8,128]{3,2,1,0:T(8,128)(2,1)} %param.9) | copy-start | bytes 786436
  37.4 4.0 %copy-start.19 = (bf16[1,128,8,128]{3,2,1,0:T(8,128)(2,1)S(1)}, bf16[1,128,8,128]{3,2,1,0:T(8,128)(2,1)}, u32[]{:S(2)}) copy-start(bf16[1,128,8,128]{3,2,1,0:T(8,128)(2,1)} %param.8) | copy-start | bytes 786436
  45.4 53.5 %all-to-all-start.2 = ((bf16[16,4,32,128]{3,2,1,0:T(8,128)(2,1)}), bf16[16,4,32,128]{3,2,1,0:T(8,128)(2,1)S(1)}, u32[]{:S(2)}, u32[]{:S(2)}) async-start(bf16[16,4,32,128]{3,2,1,0:T(8,128)(2,1)} %bitcast.7), calls=%async_computation.2 | async-start | bytes 1048576 | tf_op jit(solution)/shard_map/all_to_all | solution.py:214
  51.6 6.2 %collective-permute-start.1 = (bf16[1,4,32,128]{3,2,1,0:T(8,128)(2,1)S(1)}, bf16[1,4,32,128]{3,2,1,0:T(8,128)(2,1)S(1)}, u32[]{:S(2)}, u32[]{:S(2)}) collective-permute-start(bf16[1,4,32,128]{3,2,1,0:T(8,128)(2,1)S(1)} %get-tuple-element.1325), channel_id=1, source_target_pairs={{0,2},{1,3},{2,0},{3,1},{4,6},{5,7},{6,4},{7,5},{8,10},{9,11},{10,... | collective-permute-start | bytes 98312 | tf_op jit(solution)/shard_map/ppermute | solution.py:257
  57.9 3.6 %collective-permute-start.2 = (bf16[1,4,32,128]{3,2,1,0:T(8,128)(2,1)S(1)}, bf16[1,4,32,128]{3,2,1,0:T(8,128)(2,1)S(1)}, u32[]{:S(2)}, u32[]{:S(2)}) collective-permute-start(bf16[1,4,32,128]{3,2,1,0:T(8,128)(2,1)S(1)} %get-tuple-element.1324), channel_id=1, source_target_pairs={{0,3},{1,2},{2,1},{3,0},{4,7},{5,6},{6,5},{7,4},{8,11},{9,10},{10,... | collective-permute-start | bytes 98312 | tf_op jit(solution)/shard_map/ppermute | solution.py:257
  61.5 4.2 %collective-permute-start.3 = (bf16[1,4,32,128]{3,2,1,0:T(8,128)(2,1)S(1)}, bf16[1,4,32,128]{3,2,1,0:T(8,128)(2,1)S(1)}, u32[]{:S(2)}, u32[]{:S(2)}) collective-permute-start(bf16[1,4,32,128]{3,2,1,0:T(8,128)(2,1)S(1)} %get-tuple-element.1323), channel_id=1, source_target_pairs={{0,4},{1,5},{2,6},{3,7},{4,0},{5,1},{6,2},{7,3},{8,12},{9,13},{10,... | collective-permute-start | bytes 98312 | tf_op jit(solution)/shard_map/ppermute | solution.py:257
  65.6 3.3 %collective-permute-start.4 = (bf16[1,4,32,128]{3,2,1,0:T(8,128)(2,1)S(1)}, bf16[1,4,32,128]{3,2,1,0:T(8,128)(2,1)S(1)}, u32[]{:S(2)}, u32[]{:S(2)}) collective-permute-start(bf16[1,4,32,128]{3,2,1,0:T(8,128)(2,1)S(1)} %get-tuple-element.1322), channel_id=1, source_target_pairs={{0,5},{1,4},{2,7},{3,6},{4,1},{5,0},{6,3},{7,2},{8,13},{9,12},{10,... | collective-permute-start | bytes 98312 | tf_op jit(solution)/shard_map/ppermute | solution.py:257
  69.0 4.8 %collective-permute-start.5 = (bf16[1,4,32,128]{3,2,1,0:T(8,128)(2,1)S(1)}, bf16[1,4,32,128]{3,2,1,0:T(8,128)(2,1)S(1)}, u32[]{:S(2)}, u32[]{:S(2)}) collective-permute-start(bf16[1,4,32,128]{3,2,1,0:T(8,128)(2,1)S(1)} %get-tuple-element.1321), channel_id=1, source_target_pairs={{0,6},{1,7},{2,4},{3,5},{4,2},{5,3},{6,0},{7,1},{8,14},{9,15},{10,... | collective-permute-start | bytes 98312 | tf_op jit(solution)/shard_map/ppermute | solution.py:257
  73.8 4.2 %collective-permute-start.6 = (bf16[1,4,32,128]{3,2,1,0:T(8,128)(2,1)S(1)}, bf16[1,4,32,128]{3,2,1,0:T(8,128)(2,1)S(1)}, u32[]{:S(2)}, u32[]{:S(2)}) collective-permute-start(bf16[1,4,32,128]{3,2,1,0:T(8,128)(2,1)S(1)} %get-tuple-element.1320), channel_id=1, source_target_pairs={{0,7},{1,6},{2,5},{3,4},{4,3},{5,2},{6,1},{7,0},{8,15},{9,14},{10,... | collective-permute-start | bytes 98312 | tf_op jit(solution)/shard_map/ppermute | solution.py:257
  78.0 4.8 %collective-permute-start.7 = (bf16[1,4,32,128]{3,2,1,0:T(8,128)(2,1)S(1)}, bf16[1,4,32,128]{3,2,1,0:T(8,128)(2,1)S(1)}, u32[]{:S(2)}, u32[]{:S(2)}) collective-permute-start(bf16[1,4,32,128]{3,2,1,0:T(8,128)(2,1)S(1)} %get-tuple-element.1319), channel_id=1, source_target_pairs={{0,8},{1,9},{2,10},{3,11},{4,12},{5,13},{6,14},{7,15},{8,0},{9,1},... | collective-permute-start | bytes 98312 | tf_op jit(solution)/shard_map/ppermute | solution.py:257
  82.9 4.3 %collective-permute-start.8 = (bf16[1,4,32,128]{3,2,1,0:T(8,128)(2,1)S(1)}, bf16[1,4,32,128]{3,2,1,0:T(8,128)(2,1)S(1)}, u32[]{:S(2)}, u32[]{:S(2)}) collective-permute-start(bf16[1,4,32,128]{3,2,1,0:T(8,128)(2,1)S(1)} %get-tuple-element.1318), channel_id=1, source_target_pairs={{0,9},{1,8},{2,11},{3,10},{4,13},{5,12},{6,15},{7,14},{8,1},{9,0},... | collective-permute-start | bytes 98312 | tf_op jit(solution)/shard_map/ppermute | solution.py:257
  87.2 6.4 %collective-permute-start.9 = (bf16[1,4,32,128]{3,2,1,0:T(8,128)(2,1)S(1)}, bf16[1,4,32,128]{3,2,1,0:T(8,128)(2,1)S(1)}, u32[]{:S(2)}, u32[]{:S(2)}) collective-permute-start(bf16[1,4,32,128]{3,2,1,0:T(8,128)(2,1)S(1)} %get-tuple-element.1317), channel_id=1, source_target_pairs={{0,10},{1,11},{2,8},{3,9},{4,14},{5,15},{6,12},{7,13},{8,2},{9,3},... | collective-permute-start | bytes 98312 | tf_op jit(solution)/shard_map/ppermute | solution.py:257
  93.6 5.4 %collective-permute-start.10 = (bf16[1,4,32,128]{3,2,1,0:T(8,128)(2,1)S(1)}, bf16[1,4,32,128]{3,2,1,0:T(8,128)(2,1)S(1)}, u32[]{:S(2)}, u32[]{:S(2)}) collective-permute-start(bf16[1,4,32,128]{3,2,1,0:T(8,128)(2,1)S(1)} %get-tuple-element.1316), channel_id=1, source_target_pairs={{0,11},{1,10},{2,9},{3,8},{4,15},{5,14},{6,13},{7,12},{8,3},{9,2},... | collective-permute-start | bytes 98312 | tf_op jit(solution)/shard_map/ppermute | solution.py:257
  99.0 18.2 %all-to-all-start.1 = ((bf16[16,4,32,128]{3,2,1,0:T(8,128)(2,1)}), bf16[16,4,32,128]{3,2,1,0:T(8,128)(2,1)S(1)}, u32[]{:S(2)}, u32[]{:S(2)}) async-start(bf16[16,4,32,128]{3,2,1,0:T(8,128)(2,1)} %bitcast.4), calls=%async_computation.1 | async-start | bytes 1048576 | tf_op jit(solution)/shard_map/all_to_all | solution.py:213
  104.4 17.7 %copy-start.12 = (bf16[16,1,32,128]{3,2,1,0:T(8,128)(2,1)}, bf16[16,1,32,128]{3,2,1,0:T(8,128)(2,1)S(1)}, u32[]{:S(2)}) copy-start(bf16[16,1,32,128]{3,2,1,0:T(8,128)(2,1)S(1)} %get-tuple-element.1328) | copy-start | bytes 393220
  104.4 34.3 %copy-start.10 = (bf16[16,1,32,128]{3,2,1,0:T(8,128)(2,1)}, bf16[16,1,32,128]{3,2,1,0:T(8,128)(2,1)S(1)}, u32[]{:S(2)}) copy-start(bf16[16,1,32,128]{3,2,1,0:T(8,128)(2,1)S(1)} %get-tuple-element.1327) | copy-start | bytes 393220
  104.4 39.0 %copy-start.8 = (bf16[16,1,32,128]{3,2,1,0:T(8,128)(2,1)}, bf16[16,1,32,128]{3,2,1,0:T(8,128)(2,1)S(1)}, u32[]{:S(2)}) copy-start(bf16[16,1,32,128]{3,2,1,0:T(8,128)(2,1)S(1)} %get-tuple-element.1329) | copy-start | bytes 393220
  117.2 18.4 %all-to-all-start.3 = ((bf16[16,4,32,128]{3,2,1,0:T(8,128)(2,1)}), bf16[16,4,32,128]{3,2,1,0:T(8,128)(2,1)S(1)}, u32[]{:S(2)}, u32[]{:S(2)}) async-start(bf16[16,4,32,128]{3,2,1,0:T(8,128)(2,1)} %bitcast.11), calls=%async_computation.3 | async-start | bytes 1048576 | tf_op jit(solution)/shard_map/all_to_all | solution.py:215
  122.1 21.4 %copy-start.15 = (bf16[16,1,32,128]{3,2,1,0:T(8,128)(2,1)}, bf16[16,1,32,128]{3,2,1,0:T(8,128)(2,1)S(1)}, u32[]{:S(2)}) copy-start(bf16[16,1,32,128]{3,2,1,0:T(8,128)(2,1)S(1)} %get-tuple-element.1333) | copy-start | bytes 393220
  147.0 1.0 copy-start.13
  148.3 8.9 %copy-start.3 = (f32[512,512]{0,1:T(8,128)}, f32[512,512]{0,1:T(8,128)S(1)}, u32[]{:S(2)}) copy-start(f32[512,512]{0,1:T(8,128)S(1)} %get-tuple-element.1348) | copy-start | bytes 3145732
  149.0 1.0 copy-start.20
  151.7 18.4 %all-to-all-start.7 = ((bf16[16,4,32,128]{3,2,1,0:T(8,128)(2,1)}), bf16[16,4,32,128]{3,2,1,0:T(8,128)(2,1)S(1)}, u32[]{:S(2)}, u32[]{:S(2)}) async-start(bf16[16,4,32,128]{3,2,1,0:T(8,128)(2,1)} %pad_maximum_fusion.3), calls=%async_computation.7 | async-start | bytes 1048576 | tf_op jit(solution)/shard_map/all_to_all | solution.py:286
  155.9 1.3 copy-start.21
  155.9 1.3 copy-start.24
  158.3 1.6 copy-start.14
  160.0 2.0 copy-start.1
  160.0 1.0 copy-start.16
  160.0 1.1 copy-start.17
  162.0 12.4 %copy-start.22 = (bf16[512,128]{1,0:T(8,128)(2,1)S(1)}, bf16[512,128]{1,0:T(8,128)(2,1)}, u32[]{:S(2)}) copy-start(bf16[512,128]{1,0:T(8,128)(2,1)} %get-tuple-element.1352) | copy-start | bytes 393220
  162.0 12.4 %copy-start.23 = (bf16[512,128]{1,0:T(8,128)(2,1)S(1)}, bf16[512,128]{1,0:T(8,128)(2,1)}, u32[]{:S(2)}) copy-start(bf16[512,128]{1,0:T(8,128)(2,1)} %get-tuple-element.1358) | copy-start | bytes 393220
  162.0 12.4 %copy-start.26 = (bf16[512,128]{1,0:T(8,128)(2,1)S(1)}, bf16[512,128]{1,0:T(8,128)(2,1)}, u32[]{:S(2)}) copy-start(bf16[512,128]{1,0:T(8,128)(2,1)} %get-tuple-element.1354) | copy-start | bytes 393220
  162.0 12.4 %copy-start.27 = (bf16[512,128]{1,0:T(8,128)(2,1)S(1)}, bf16[512,128]{1,0:T(8,128)(2,1)}, u32[]{:S(2)}) copy-start(bf16[512,128]{1,0:T(8,128)(2,1)} %get-tuple-element.1356) | copy-start | bytes 393220
  170.2 18.4 %all-to-all-start.6 = ((bf16[16,4,32,128]{3,2,1,0:T(8,128)(2,1)}), bf16[16,4,32,128]{3,2,1,0:T(8,128)(2,1)S(1)}, u32[]{:S(2)}, u32[]{:S(2)}) async-start(bf16[16,4,32,128]{3,2,1,0:T(8,128)(2,1)} %pad_maximum_fusion.2), calls=%async_computation.6 | async-start | bytes 1048576 | tf_op jit(solution)/shard_map/all_to_all | solution.py:283
  188.6 18.4 %all-to-all-start.4 = ((bf16[16,4,32,128]{3,2,1,0:T(8,128)(2,1)}), bf16[16,4,32,128]{3,2,1,0:T(8,128)(2,1)S(1)}, u32[]{:S(2)}, u32[]{:S(2)}) async-start(bf16[16,4,32,128]{3,2,1,0:T(8,128)(2,1)} %pad_maximum_fusion), calls=%async_computation.4 | async-start | bytes 1048576 | tf_op jit(solution)/shard_map/all_to_all | solution.py:244
  192.8 2.5 %copy-start.11 = (bf16[16,1,32,128]{3,2,1,0:T(8,128)(2,1)S(1)}, bf16[16,1,32,128]{3,2,1,0:T(8,128)(2,1)}, u32[]{:S(2)}) copy-start(bf16[16,1,32,128]{3,2,1,0:T(8,128)(2,1)} %copy-done.10) | copy-start | bytes 393220
  196.2 1.0 copy-start.2
  196.2 1.1 copy-start.7
  207.1 28.4 %all-to-all-start.5 = ((bf16[16,4,32,128]{3,2,1,0:T(8,128)(2,1)}), bf16[16,4,32,128]{3,2,1,0:T(8,128)(2,1)S(1)}, u32[]{:S(2)}, u32[]{:S(2)}) async-start(bf16[16,4,32,128]{3,2,1,0:T(8,128)(2,1)} %pad_maximum_fusion.1), calls=%async_computation.5 | async-start | bytes 1048576 | tf_op jit(solution)/shard_map/all_to_all | solution.py:280
  231.7 3.2 %copy-start.5 = (bf16[1,128,8,128]{3,2,1,0:T(8,128)(2,1)S(1)}, bf16[1,128,8,128]{3,2,1,0:T(8,128)(2,1)}, u32[]{:S(2)}) copy-start(bf16[1,128,8,128]{3,2,1,0:T(8,128)(2,1)} %param.13) | copy-start | bytes 786436
  (6 other events, 4.8 us)
